TPU v7x, 256 devices: a whole 4x4x8 slice. The times are simulated.
256 devices in a mesh: gx: 16 (over x_hi, z), gy: 8 (over y, core), gz: 2 (over x_lo).
Axes of the slice: x: 4 (x_hi: 2, x_lo: 2; x = x_hi * 2 + x_lo), y: 4, z: 8, core: 2. Of those that a mesh axis runs over, the one named last changes fastest.
Arguments:
- features: bfloat16 [512, 128, 256], P(('gx', 'gy', 'gz')), may hold values from -0.59765625 to 0.59765625
- cotangent: bfloat16 [512, 128, 256], P(('gx', 'gy', 'gz')), may hold values from -6 to 6
- positions: bfloat16 [512, 3, 128], P(('gx', 'gy', 'gz')), may hold values from 0 to 4
- element_types: int32 [512, 128], P(('gx', 'gy', 'gz')), may hold values from 0 to 7
- charge_table: float32 [8], replicated, may hold values from -1.5 to 1.5
- partners: int32 [512, 24], P(('gx', 'gy', 'gz')), may hold values from 0 to 511, as said below
- tile_real_flags: int32 [512, 24], P(('gx', 'gy', 'gz')), may hold values from 0 to 1, as said below
Outputs:
- grad_features: float32 [512, 128, 256], P(('gx', 'gy', 'gz'))
- grad_positions: float32 [512, 3, 128], P(('gx', 'gy', 'gz'))
Inputs may be any that keep to these rules, and one draw needn't show every extreme that they name: `partners`: clusters are numbered by device, 2 a device, device number (gx index * size of gy + gy index) * size of gz + gz index; a cluster's local index is 0 or 1. Every entry, padding included, names the other cluster of the same device, or the cluster with local index 0 on the device whose lateral index gx index * size of gy + gy index is one higher (cyclically) and whose gz index is the same, or either cluster of the device one step higher along gz. The live tiles of one cluster name distinct clusters. `tile_real_flags`: A cluster has at most min(24, 4) live tiles, and some cluster has exactly that many.
All inputs are finite; a program needn't handle non-finite values.
Results may differ from a plain program's by a relative error of at most 0.0066.
Values may be sent and summed in bfloat16 or wider, within the bound.
A program may use at most 64 MiB of HBM per device.

v0:
```python
import math

import jax
import jax.numpy as jnp
from jax import lax
from jax.sharding import PartitionSpec as P

coupling_strength = 0.0625
screening = 0.3
soften = 1.0


def from_behind(block, axis, distance):
    devices = range(lax.axis_size(axis))
    route = [((i - distance) % len(devices), i) for i in devices]
    return lax.ppermute(block, axis, route)


def passed_along(value, axis, by):
    count = lax.axis_size(axis)
    pairs = [(i, i + by) for i in range(count) if 0 <= i + by < count]
    return lax.ppermute(value, axis, pairs)


def pairwise_terms(
    nearby_features,
    nearby_cotangent,
    remote_features,
    remote_cotangent,
    nearby_position_charge,
    remote_position_charge,
    tile_real_mask,
):
    near_pos = nearby_position_charge.astype(jnp.float32)
    far_pos = remote_position_charge.astype(jnp.float32)
    offsets = near_pos[:, :3, :, None] - far_pos[:, :3, None, :]
    radius = jnp.sqrt(jnp.sum(offsets * offsets, axis=1) + soften)
    atom_charges = near_pos[:, 3, :, None] * far_pos[:, 3, None, :]
    screen = lax.erfc(screening * radius)
    scaled_terms = coupling_strength * tile_real_mask[:, None, None] * atom_charges
    kernel = (scaled_terms * screen / radius).astype(jnp.bfloat16)
    grad_near = jnp.einsum(
        "txy,tyc->txc", kernel, remote_cotangent, preferred_element_type=jnp.float32
    )
    grad_far = jnp.einsum(
        "txy,txc->tyc", kernel, nearby_cotangent, preferred_element_type=jnp.float32
    )
    pair_sum = jnp.einsum(
        "txc,tyc->txy", nearby_cotangent, remote_features, preferred_element_type=jnp.float32
    )
    pair_sum = pair_sum + jnp.einsum(
        "txc,tyc->txy", nearby_features, remote_cotangent, preferred_element_type=jnp.float32
    )
    slope_term = (
        -(2.0 * screening / math.sqrt(math.pi))
        * jnp.exp(-screening * screening * radius * radius)
        / radius
        - screen / (radius * radius)
    ) / radius
    weight = scaled_terms * slope_term * pair_sum
    moved = weight[:, None, :, :] * offsets
    return (grad_near, grad_far, jnp.sum(moved, axis=3), -jnp.sum(moved, axis=2))


def pick_rows(row_ids, pool):
    selector = (row_ids[:, None] == jnp.arange(pool.shape[0], dtype=jnp.int32)[None, :]).astype(
        pool.dtype
    )
    return jnp.einsum("tp,p...->t...", selector, pool, preferred_element_type=jnp.float32).astype(
        pool.dtype
    )


def spread_rows(row_ids, pool_size, values):
    selector = (row_ids[:, None] == jnp.arange(pool_size, dtype=jnp.int32)[None, :]).astype(
        jnp.float32
    )
    return jnp.einsum("tp,t...->p...", selector, values, precision=lax.Precision.HIGHEST)


def per_device(
    features, cotangent, positions, element_types, charge_table, partners, tile_real_flags
):
    clusters = features.shape[0]
    cluster_totals = partners.shape[1]
    elements = charge_table.shape[0]
    matches = element_types[:, :, None] == jnp.arange(elements, dtype=jnp.int32)
    charge = jnp.sum(jnp.where(matches, charge_table, 0.0), axis=2).astype(jnp.bfloat16)
    position_charge = jnp.concatenate([positions, charge[:, None, :]], axis=1)
    side_send = (features, cotangent, position_charge)
    upper_send = (features, cotangent, position_charge)
    lateral_in = from_behind((side_send[0], side_send[1], side_send[2]), ("gx", "gy"), -1)
    upper_in = passed_along((upper_send[0], upper_send[1], upper_send[2]), "gz", -1)
    side_count = lateral_in[0].shape[0]
    upper_count = upper_in[0].shape[0]
    feat_pool = jnp.concatenate([features, lateral_in[0], upper_in[0]], axis=0)
    cot_pool = jnp.concatenate([cotangent, lateral_in[1], upper_in[1]], axis=0)
    posq_pool = jnp.concatenate([position_charge, lateral_in[2], upper_in[2]], axis=0)
    lateral = lax.axis_index(("gx", "gy"))
    height = lax.axis_index("gz")
    levels = lax.axis_size("gz")
    device = partners // clusters
    local_index = partners % clusters
    is_side = device // levels != lateral
    is_upper = device % levels != height
    pool_slot = jnp.where(
        is_side,
        clusters + local_index,
        jnp.where(is_upper, clusters + side_count + local_index, local_index),
    )
    pool_size = clusters + side_count + upper_count
    start_feat = jnp.zeros((pool_size,) + features.shape[1:], jnp.float32)
    start_pos = jnp.zeros((pool_size,) + positions.shape[1:], jnp.float32)
    live_grid = tile_real_flags.astype(jnp.float32)

    def cluster_step(totals, inputs):
        acc_feat, acc_pos = totals
        near_feat, near_cot, near_posq, remote_cluster_rows, tile_real_mask = inputs
        pairwise_gradient = pairwise_terms(
            jnp.broadcast_to(near_feat[None], (cluster_totals,) + near_feat.shape),
            jnp.broadcast_to(near_cot[None], (cluster_totals,) + near_cot.shape),
            pick_rows(remote_cluster_rows, feat_pool),
            pick_rows(remote_cluster_rows, cot_pool),
            jnp.broadcast_to(near_posq[None], (cluster_totals,) + near_posq.shape),
            pick_rows(remote_cluster_rows, posq_pool),
            tile_real_mask,
        )
        acc_feat = acc_feat + spread_rows(remote_cluster_rows, pool_size, pairwise_gradient[1])
        acc_pos = acc_pos + spread_rows(remote_cluster_rows, pool_size, pairwise_gradient[3])
        return (
            (acc_feat, acc_pos),
            (jnp.sum(pairwise_gradient[0], axis=0), jnp.sum(pairwise_gradient[2], axis=0)),
        )

    (grad_feat, grad_pos), (near_feat_rows, near_pos_rows) = lax.scan(
        cluster_step,
        (start_feat, start_pos),
        (features, cotangent, position_charge, pool_slot, live_grid),
    )
    extra_rows = pool_size - clusters
    grad_feat = grad_feat + jnp.pad(near_feat_rows, ((0, extra_rows), (0, 0), (0, 0)))
    grad_pos = grad_pos + jnp.pad(near_pos_rows, ((0, extra_rows), (0, 0), (0, 0)))
    side_back = from_behind(
        (
            grad_feat[clusters : clusters + side_count].astype(jnp.bfloat16),
            grad_pos[clusters : clusters + side_count].astype(jnp.bfloat16),
        ),
        ("gx", "gy"),
        1,
    )
    upper_back = passed_along(
        (
            grad_feat[clusters + side_count :].astype(jnp.bfloat16),
            grad_pos[clusters + side_count :].astype(jnp.bfloat16),
        ),
        "gz",
        1,
    )
    side_feat = side_back[0].astype(jnp.float32)
    side_pos = side_back[1].astype(jnp.float32)
    upper_feat = upper_back[0].astype(jnp.float32)
    upper_pos = upper_back[1].astype(jnp.float32)
    own_feat = grad_feat[:clusters]
    own_pos = grad_pos[:clusters]
    own_feat = own_feat + side_feat
    own_pos = own_pos + side_pos
    own_feat = own_feat + upper_feat
    own_pos = own_pos + upper_pos
    return (own_feat, own_pos)


def solution(mesh):
    return jax.shard_map(
        per_device,
        mesh=mesh,
        in_specs=(
            P(("gx", "gy", "gz"), None, None),
            P(("gx", "gy", "gz"), None, None),
            P(("gx", "gy", "gz"), None, None),
            P(("gx", "gy", "gz"), None),
            P(),
            P(("gx", "gy", "gz"), None),
            P(("gx", "gy", "gz"), None),
        ),
        out_specs=(P(("gx", "gy", "gz"), None, None), P(("gx", "gy", "gz"), None, None)),
        check_vma=False,
    )
```

profile of v0, /device:TPU:2, one launch (start us, length us, event | category | flops | bytes accessed | tf_op | source)
XLA Modules:
  0.0 76.3 jit_solution(12089288304585167267)
XLA Ops:
  0.6 0.7 copy.61
  1.3 0.8 %select_reduce_fusion = bf16[2,128]{1,0:T(2,128)(2,1)S(1)} fusion(f32[8]{0:T(128)} %param.13, s32[2,128]{1,0:T(2,128)} %param.12), kind=kLoop, calls=%fused_computation.78 | loop fusion | flops 5888 | bytes 1568 | tf_op jit(solution)/shard_map/reduce_sum | solution.py:88
  2.1 9.4 %collective-permute-start = (bf16[2,4,128]{2,0,1:T(2,128)(2,1)S(1)}, bf16[2,4,128]{2,0,1:T(2,128)(2,1)S(1)}, u32[]{:S(2)}, u32[]{:S(2)}) collective-permute-start(bf16[2,4,128]{2,0,1:T(2,128)(2,1)S(1)} %copy.65), channel_id=1, source_target_pairs={{2,0},{4,2},{6,4},{8,6},{10,8},{12,10},{14,12},{16,14},{18,16},{20... | collective-permute-start | bytes 6152 | tf_op jit(solution)/shard_map/ppermute | solution.py:16
  11.5 3.3 %collective-permute-start.1 = (bf16[2,4,128]{2,0,1:T(2,128)(2,1)S(1)}, bf16[2,4,128]{2,0,1:T(2,128)(2,1)S(1)}, u32[]{:S(2)}, u32[]{:S(2)}) collective-permute-start(bf16[2,4,128]{2,0,1:T(2,128)(2,1)S(1)} %copy.65), channel_id=1, source_target_pairs={{1,0},{3,2},{5,4},{7,6},{9,8},{11,10},{13,12},{15,14},{17,16},{19,... | collective-permute-start | bytes 6152 | tf_op jit(solution)/shard_map/ppermute | solution.py:22
  14.8 1.0 %copy.68 = bf16[2,128,256]{2,0,1:T(2,128)(2,1)S(1)} copy(bf16[2,128,256]{2,1,0:T(8,128)(2,1)} %param.9) | data formatting | bytes 262144 | tf_op args[0]
  16.0 1.9 %collective-permute-start.3 = (bf16[2,128,256]{2,0,1:T(2,128)(2,1)S(1)}, bf16[2,128,256]{2,0,1:T(2,128)(2,1)S(1)}, u32[]{:S(2)}, u32[]{:S(2)}) collective-permute-start(bf16[2,128,256]{2,0,1:T(2,128)(2,1)S(1)} %copy.68), channel_id=1, source_target_pairs={{1,0},{3,2},{5,4},{7,6},{9,8},{11,10},{13,12},{15,14},{17,16},{19,... | collective-permute-start | bytes 393224 | tf_op jit(solution)/shard_map/ppermute | solution.py:22
  17.9 1.0 %copy.71 = bf16[2,128,256]{2,0,1:T(2,128)(2,1)S(1)} copy(bf16[2,128,256]{2,1,0:T(8,128)(2,1)} %param.10) | data formatting | bytes 262144 | tf_op args[1]
  19.1 1.3 %compare_select_fusion.1 = s32[2,24]{1,0:T(2,128)} fusion(s32[2,24]{1,0:T(2,128)} %param.14, s32[]{:T(128)S(6)} %axis_index.38, s32[]{:T(128)S(6)} %add.62), kind=kLoop, calls=%fused_computation.86 | loop fusion | flops 2112 | bytes 392 | tf_op jit(solution)/shard_map/jit(_where)/select_n | solution.py:106
  21.0 1.4 %collective-permute-start.5 = (bf16[2,128,256]{2,0,1:T(2,128)(2,1)S(1)}, bf16[2,128,256]{2,0,1:T(2,128)(2,1)S(1)}, u32[]{:S(2)}, u32[]{:S(2)}) collective-permute-start(bf16[2,128,256]{2,0,1:T(2,128)(2,1)S(1)} %copy.71), channel_id=1, source_target_pairs={{1,0},{3,2},{5,4},{7,6},{9,8},{11,10},{13,12},{15,14},{17,16},{19,... | collective-permute-start | bytes 393224 | tf_op jit(solution)/shard_map/ppermute | solution.py:22
  22.5 1.2 %pad_maximum_fusion = bf16[6,128,256]{2,0,1:T(8,128)(2,1)} fusion(bf16[2,128,256]{2,0,1:T(2,128)(2,1)S(1)} %collective-permute-done.3, bf16[2,128,256]{2,0,1:T(2,128)(2,1)S(1)} %collective-permute-done.2, bf16[2,128,256]{2,0,1:T(2,128)(2,1)S(1)} %copy.68), kind=kLoop, calls=%fused_computation.72 | loop fusion | flops 1179648 | bytes 786432 | tf_op jit(solution)/shard_map/concatenate | solution.py:96
  23.8 2.2 %collective-permute-done.5 = bf16[2,128,256]{2,0,1:T(2,128)(2,1)S(1)} collective-permute-done((bf16[2,128,256]{2,0,1:T(2,128)(2,1)S(1)}, bf16[2,128,256]{2,0,1:T(2,128)(2,1)S(1)}, u32[]{:S(2)}, u32[]{:S(2)}) %collective-permute-start.5) | collective-permute-done | bytes 131104 | tf_op jit(solution)/shard_map/ppermute | solution.py:22
  26.0 1.2 %pad_maximum_fusion.1 = bf16[6,128,256]{2,0,1:T(8,128)(2,1)} fusion(bf16[2,128,256]{2,0,1:T(2,128)(2,1)S(1)} %collective-permute-done.5, bf16[2,128,256]{2,0,1:T(2,128)(2,1)S(1)} %collective-permute-done.4, bf16[2,128,256]{2,0,1:T(2,128)(2,1)S(1)} %copy.71), kind=kLoop, calls=%fused_computation.73 | loop fusion | flops 1179648 | bytes 786432 | tf_op jit(solution)/shard_map/concatenate | solution.py:97
  27.2 34.8 %while.17 = (s32[]{:T(128)}, f32[6,128,256]{2,0,1:T(8,128)S(1)}, f32[6,3,128]{2,0,1:T(8,128)S(1)}, f32[2,128,256]{2,1,0:T(8,128)}, f32[2,3,128]{2,0,1:T(2,128)},...) while((s32[]{:T(128)}, f32[6,128,256]{2,0,1:T(8,128)S(1)}, ...), condition=%wide.region_5.6_spmd.clone, body=%wide.region_1.5_spmd.clone.sunk | while | flops 923325760 | bytes 38254452 | solution.py:135
  28.8 4.0 %divide_convert_fusion.2 = (bf16[24,128,128]{2,1,0:T(8,128)(2,1)S(1)}, f32[24,128,128]{2,1,0:T(8,128)S(1)}) fusion(f32[24,128,128]{2,1,0:T(8,128)S(1)} %fusion.114, f32[24,128]{1,0:T(8,128)S(1)} %slice_bitcast_fusion.7, f32[128]{0:T(128)S(1)} %slice_bitcast_fusion.8, f32[24]{0:T(128)S(1)} %fusion.115), kind=kLoop, calls=%fused_computation.21.clone.1 | loop fusion | flops 26345472 | bytes 3945056 | tf_op jit(solution)/shard_map/while/body/eval_jaxpr/convert_element_type | solution.py:41
  35.5 1.8 %add_multiply_fusion.2 = f32[24,128,128]{2,1,0:T(8,128)S(1)} fusion(f32[24,128,128]{2,1,0:T(8,128)S(1)} %fusion.118, f32[24,128,128]{2,1,0:T(8,128)S(1)} %get-tuple-element.246, bf16[24,128,256]{2,0,1:T(8,128)(2,1)S(1)} %convolution_convert_fusion.6, f32[24,128,128]{2,1,0:T(8,128)S(1)} %fusion.114, bf16[128,256]{1,0:T(8,128)(2,1)S(1)} %get-tuple-element.244, ...), kind=kOutput, calls=%fused_computation.20.clone.1 | convolution fusion | flops 206831616 | bytes 7942752 | tf_op jit(solution)/shard_map/while/body/eval_jaxpr/txc,tyc->txy/dot_general | solution.py:48
  37.3 1.0 %fusion.119 = (f32[3,128]{1,0:T(4,128)S(1)}, f32[24,3,128]{2,1,0:T(4,128)S(1)}) fusion(f32[24,128,128]{2,1,0:T(8,128)S(1)} %add_multiply_fusion.2, f32[24,3,128]{2,1,0:T(4,128)S(1)} %copy.112, f32[3,128]{1,0:T(4,128)S(1)} %slice_bitcast_fusion.6), kind=kLoop, calls=%fused_computation.2.clone.1 | loop fusion | flops 4708992 | bytes 1649664 | tf_op jit(solution)/shard_map/while/body/eval_jaxpr/reduce_sum | solution.py:132
  38.5 1.3 %dynamic_update_slice.14 = f32[2,3,128]{2,0,1:T(2,128)} dynamic-update-slice(f32[2,3,128]{2,0,1:T(2,128)} %get-tuple-element.268, f32[1,3,128]{2,0,1:T(1,128)S(1)} %copy.113, s32[]{:T(128)} %get-tuple-element.264, s32[]{:T(128)} %constant.136.clone.1..sunk, s32[]{:T(128)} %constant.136.clone.1..sunk) | dynamic-update-slice | bytes 3076 | tf_op jit(solution)/shard_map/while/body/jit(dynamic_update_index_in_dim)/dynamic_update_slice | solution.py:135
  40.4 3.0 %fusion.117 = f32[6,128,256]{2,0,1:T(8,128)S(1)} fusion(f32[24,128,256]{2,1,0:T(8,128)S(1)} %fusion.116, f32[6,128,256]{2,0,1:T(8,128)S(1)} %get-tuple-element.265, pred[]{:T(512)S(6)} %compare.11, s32[24]{0:T(128)S(1)} %fusion.111), kind=kOutput, calls=%fused_computation.41.clone.1 | convolution fusion | flops 57016464 | bytes 4718689 | tf_op jit(solution)/shard_map/while/body/eval_jaxpr/tp,t...->p.../dot_general | solution.py:78
  43.5 1.2 %fusion.120 = f32[2,128,256]{2,1,0:T(8,128)} fusion(f32[2,128,256]{2,1,0:T(8,128)} %get-tuple-element.267, s32[]{:T(128)} %get-tuple-element.264, bf16[24,128,128]{2,1,0:T(8,128)(2,1)S(1)} %get-tuple-element.243, bf16[24,128,256]{2,0,1:T(8,128)(2,1)S(1)} %convolution_convert_fusion.5), kind=kOutput, calls=%fused_computation.43.clone.1 | convolution fusion | flops 201326592 | bytes 2490880 | tf_op jit(solution)/shard_map/while/body/eval_jaxpr/txy,tyc->txc/dot_general | solution.py:42
  46.2 4.0 %divide_convert_fusion.2 = (bf16[24,128,128]{2,1,0:T(8,128)(2,1)S(1)}, f32[24,128,128]{2,1,0:T(8,128)S(1)}) fusion(f32[24,128,128]{2,1,0:T(8,128)S(1)} %fusion.114, f32[24,128]{1,0:T(8,128)S(1)} %slice_bitcast_fusion.7, f32[128]{0:T(128)S(1)} %slice_bitcast_fusion.8, f32[24]{0:T(128)S(1)} %fusion.115), kind=kLoop, calls=%fused_computation.21.clone.1 | loop fusion | flops 26345472 | bytes 3945056 | tf_op jit(solution)/shard_map/while/body/eval_jaxpr/convert_element_type | solution.py:41
  52.9 1.8 %add_multiply_fusion.2 = f32[24,128,128]{2,1,0:T(8,128)S(1)} fusion(f32[24,128,128]{2,1,0:T(8,128)S(1)} %fusion.118, f32[24,128,128]{2,1,0:T(8,128)S(1)} %get-tuple-element.246, bf16[24,128,256]{2,0,1:T(8,128)(2,1)S(1)} %convolution_convert_fusion.6, f32[24,128,128]{2,1,0:T(8,128)S(1)} %fusion.114, bf16[128,256]{1,0:T(8,128)(2,1)S(1)} %get-tuple-element.244, ...), kind=kOutput, calls=%fused_computation.20.clone.1 | convolution fusion | flops 206831616 | bytes 7942752 | tf_op jit(solution)/shard_map/while/body/eval_jaxpr/txc,tyc->txy/dot_general | solution.py:48
  54.7 1.0 %fusion.119 = (f32[3,128]{1,0:T(4,128)S(1)}, f32[24,3,128]{2,1,0:T(4,128)S(1)}) fusion(f32[24,128,128]{2,1,0:T(8,128)S(1)} %add_multiply_fusion.2, f32[24,3,128]{2,1,0:T(4,128)S(1)} %copy.112, f32[3,128]{1,0:T(4,128)S(1)} %slice_bitcast_fusion.6), kind=kLoop, calls=%fused_computation.2.clone.1 | loop fusion | flops 4708992 | bytes 1649664 | tf_op jit(solution)/shard_map/while/body/eval_jaxpr/reduce_sum | solution.py:132
  55.9 1.3 %dynamic_update_slice.14 = f32[2,3,128]{2,0,1:T(2,128)} dynamic-update-slice(f32[2,3,128]{2,0,1:T(2,128)} %get-tuple-element.268, f32[1,3,128]{2,0,1:T(1,128)S(1)} %copy.113, s32[]{:T(128)} %get-tuple-element.264, s32[]{:T(128)} %constant.136.clone.1..sunk, s32[]{:T(128)} %constant.136.clone.1..sunk) | dynamic-update-slice | bytes 3076 | tf_op jit(solution)/shard_map/while/body/jit(dynamic_update_index_in_dim)/dynamic_update_slice | solution.py:135
  57.8 3.0 %fusion.117 = f32[6,128,256]{2,0,1:T(8,128)S(1)} fusion(f32[24,128,256]{2,1,0:T(8,128)S(1)} %fusion.116, f32[6,128,256]{2,0,1:T(8,128)S(1)} %get-tuple-element.265, pred[]{:T(512)S(6)} %compare.11, s32[24]{0:T(128)S(1)} %fusion.111), kind=kOutput, calls=%fused_computation.41.clone.1 | convolution fusion | flops 57016464 | bytes 4718689 | tf_op jit(solution)/shard_map/while/body/eval_jaxpr/tp,t...->p.../dot_general | solution.py:78
  60.9 1.2 %fusion.120 = f32[2,128,256]{2,1,0:T(8,128)} fusion(f32[2,128,256]{2,1,0:T(8,128)} %get-tuple-element.267, s32[]{:T(128)} %get-tuple-element.264, bf16[24,128,128]{2,1,0:T(8,128)(2,1)S(1)} %get-tuple-element.243, bf16[24,128,256]{2,0,1:T(8,128)(2,1)S(1)} %convolution_convert_fusion.5), kind=kOutput, calls=%fused_computation.43.clone.1 | convolution fusion | flops 201326592 | bytes 2490880 | tf_op jit(solution)/shard_map/while/body/eval_jaxpr/txy,tyc->txc/dot_general | solution.py:42
  62.0 0.7 fusion.58
  62.8 1.3 %collective-permute-start.9 = (bf16[2,3,128]{2,0,1:T(2,128)(2,1)S(1)}, bf16[2,3,128]{2,0,1:T(2,128)(2,1)S(1)}, u32[]{:S(2)}, u32[]{:S(2)}) collective-permute-start(bf16[2,3,128]{2,0,1:T(2,128)(2,1)S(1)} %get-tuple-element.157), channel_id=1, source_target_pairs={{0,1},{2,3},{4,5},{6,7},{8,9},{10,11},{12,13},{14,15},{16,17},{18,... | collective-permute-start | bytes 4616 | tf_op jit(solution)/shard_map/ppermute | solution.py:22
  64.1 1.2 %fusion.59 = (bf16[6,128,256]{2,1,0:T(8,128)(2,1)S(1)}, f32[6,128,256]{2,1,0:T(8,128)S(1)}) fusion(f32[2,128,256]{2,1,0:T(8,128)} %get-tuple-element.73, f32[6,128,256]{2,0,1:T(8,128)S(1)} %get-tuple-element.72), kind=kLoop, calls=%fused_computation.97 | loop fusion | flops 393216 | bytes 2228224 | tf_op jit(solution)/shard_map/convert.3
  65.8 1.3 %collective-permute-start.7 = (bf16[2,128,256]{2,1,0:T(8,128)(2,1)S(1)}, bf16[2,128,256]{2,1,0:T(8,128)(2,1)S(1)}, u32[]{:S(2)}, u32[]{:S(2)}) collective-permute-start(bf16[2,128,256]{2,1,0:T(8,128)(2,1)S(1)} %get-tuple-element.155), channel_id=1, source_target_pairs={{0,1},{2,3},{4,5},{6,7},{8,9},{10,11},{12,13},{14,15},{16,17},{18,... | collective-permute-start | bytes 393224 | tf_op jit(solution)/shard_map/ppermute | solution.py:22
  67.1 4.4 %collective-permute-done.8 = bf16[2,3,128]{2,0,1:T(2,128)(2,1)S(1)} collective-permute-done((bf16[2,3,128]{2,0,1:T(2,128)(2,1)S(1)}, bf16[2,3,128]{2,0,1:T(2,128)(2,1)S(1)}, u32[]{:S(2)}, u32[]{:S(2)}) %collective-permute-start.8) | collective-permute-done | bytes 1568 | tf_op jit(solution)/shard_map/ppermute | solution.py:16
  72.1 3.4 %collective-permute-done.6 = bf16[2,128,256]{2,1,0:T(8,128)(2,1)S(1)} collective-permute-done((bf16[2,128,256]{2,1,0:T(8,128)(2,1)S(1)}, bf16[2,128,256]{2,1,0:T(8,128)(2,1)S(1)}, u32[]{:S(2)}, u32[]{:S(2)}) %collective-permute-start.6) | collective-permute-done | bytes 131104 | tf_op jit(solution)/shard_map/ppermute | solution.py:16
  75.6 0.7 fusion.55
  (81 shorter events, 11.8 us)
Async XLA Ops:
  2.1 18.9 %collective-permute-start = (bf16[2,4,128]{2,0,1:T(2,128)(2,1)S(1)}, bf16[2,4,128]{2,0,1:T(2,128)(2,1)S(1)}, u32[]{:S(2)}, u32[]{:S(2)}) collective-permute-start(bf16[2,4,128]{2,0,1:T(2,128)(2,1)S(1)} %copy.65), channel_id=1, source_target_pairs={{2,0},{4,2},{6,4},{8,6},{10,8},{12,10},{14,12},{16,14},{18,16},{20... | collective-permute-start | bytes 6152 | tf_op jit(solution)/shard_map/ppermute | solution.py:16
  11.5 11.0 %collective-permute-start.1 = (bf16[2,4,128]{2,0,1:T(2,128)(2,1)S(1)}, bf16[2,4,128]{2,0,1:T(2,128)(2,1)S(1)}, u32[]{:S(2)}, u32[]{:S(2)}) collective-permute-start(bf16[2,4,128]{2,0,1:T(2,128)(2,1)S(1)} %copy.65), channel_id=1, source_target_pairs={{1,0},{3,2},{5,4},{7,6},{9,8},{11,10},{13,12},{15,14},{17,16},{19,... | collective-permute-start | bytes 6152 | tf_op jit(solution)/shard_map/ppermute | solution.py:22
  15.9 6.6 %collective-permute-start.2 = (bf16[2,128,256]{2,0,1:T(2,128)(2,1)S(1)}, bf16[2,128,256]{2,0,1:T(2,128)(2,1)S(1)}, u32[]{:S(2)}, u32[]{:S(2)}) collective-permute-start(bf16[2,128,256]{2,0,1:T(2,128)(2,1)S(1)} %copy.68), channel_id=1, source_target_pairs={{2,0},{4,2},{6,4},{8,6},{10,8},{12,10},{14,12},{16,14},{18,16},{20... | collective-permute-start | bytes 393224 | tf_op jit(solution)/shard_map/ppermute | solution.py:16
  16.0 6.6 %collective-permute-start.3 = (bf16[2,128,256]{2,0,1:T(2,128)(2,1)S(1)}, bf16[2,128,256]{2,0,1:T(2,128)(2,1)S(1)}, u32[]{:S(2)}, u32[]{:S(2)}) collective-permute-start(bf16[2,128,256]{2,0,1:T(2,128)(2,1)S(1)} %copy.68), channel_id=1, source_target_pairs={{1,0},{3,2},{5,4},{7,6},{9,8},{11,10},{13,12},{15,14},{17,16},{19,... | collective-permute-start | bytes 393224 | tf_op jit(solution)/shard_map/ppermute | solution.py:22
  19.0 4.8 %collective-permute-start.4 = (bf16[2,128,256]{2,0,1:T(2,128)(2,1)S(1)}, bf16[2,128,256]{2,0,1:T(2,128)(2,1)S(1)}, u32[]{:S(2)}, u32[]{:S(2)}) collective-permute-start(bf16[2,128,256]{2,0,1:T(2,128)(2,1)S(1)} %copy.71), channel_id=1, source_target_pairs={{2,0},{4,2},{6,4},{8,6},{10,8},{12,10},{14,12},{16,14},{18,16},{20... | collective-permute-start | bytes 393224 | tf_op jit(solution)/shard_map/ppermute | solution.py:16
  21.0 5.0 %collective-permute-start.5 = (bf16[2,128,256]{2,0,1:T(2,128)(2,1)S(1)}, bf16[2,128,256]{2,0,1:T(2,128)(2,1)S(1)}, u32[]{:S(2)}, u32[]{:S(2)}) collective-permute-start(bf16[2,128,256]{2,0,1:T(2,128)(2,1)S(1)} %copy.71), channel_id=1, source_target_pairs={{1,0},{3,2},{5,4},{7,6},{9,8},{11,10},{13,12},{15,14},{17,16},{19,... | collective-permute-start | bytes 393224 | tf_op jit(solution)/shard_map/ppermute | solution.py:22
  27.2 5.6 %copy-start.4 = (f32[2,24]{1,0:T(2,128)}, f32[2,24]{1,0:T(2,128)S(1)}, u32[]{:S(2)}) copy-start(f32[2,24]{1,0:T(2,128)S(1)} %get-tuple-element.285) | copy-start | bytes 580 | tf_op jit(solution)/shard_map/while
  28.8 4.0 %copy-start.1 = (bf16[6,128,256]{2,0,1:T(8,128)(2,1)S(1)}, bf16[6,128,256]{2,0,1:T(8,128)(2,1)}, u32[]{:S(2)}) copy-start(bf16[6,128,256]{2,0,1:T(8,128)(2,1)} %get-tuple-element.291) | copy-start | bytes 1179652 | tf_op jit(solution)/shard_map/while
  32.8 0.9 %copy-start.2 = (bf16[2,128,256]{2,1,0:T(8,128)(2,1)S(1)}, bf16[2,128,256]{2,1,0:T(8,128)(2,1)}, u32[]{:S(2)}) copy-start(bf16[2,128,256]{2,1,0:T(8,128)(2,1)} %get-tuple-element.288) | copy-start | bytes 393220 | tf_op jit(solution)/shard_map/while
  32.8 1.0 %copy-start.3 = (bf16[2,128,256]{2,1,0:T(8,128)(2,1)S(1)}, bf16[2,128,256]{2,1,0:T(8,128)(2,1)}, u32[]{:S(2)}) copy-start(bf16[2,128,256]{2,1,0:T(8,128)(2,1)} %get-tuple-element.290) | copy-start | bytes 393220 | tf_op jit(solution)/shard_map/while
  33.8 1.0 %copy-start = (bf16[6,128,256]{2,0,1:T(8,128)(2,1)S(1)}, bf16[6,128,256]{2,0,1:T(8,128)(2,1)}, u32[]{:S(2)}) copy-start(bf16[6,128,256]{2,0,1:T(8,128)(2,1)} %get-tuple-element.289) | copy-start | bytes 1179652 | tf_op jit(solution)/shard_map/while
  43.5 1.2 %copy-start.5 = (f32[2,24]{1,0:T(2,128)S(1)}, f32[2,24]{1,0:T(2,128)}, u32[]{:S(2)}) copy-start(f32[2,24]{1,0:T(2,128)} %copy-done.4) | copy-start | bytes 580 | tf_op jit(solution)/shard_map/while
  44.6 5.6 %copy-start.4 = (f32[2,24]{1,0:T(2,128)}, f32[2,24]{1,0:T(2,128)S(1)}, u32[]{:S(2)}) copy-start(f32[2,24]{1,0:T(2,128)S(1)} %get-tuple-element.285) | copy-start | bytes 580 | tf_op jit(solution)/shard_map/while
  46.2 4.0 %copy-start.1 = (bf16[6,128,256]{2,0,1:T(8,128)(2,1)S(1)}, bf16[6,128,256]{2,0,1:T(8,128)(2,1)}, u32[]{:S(2)}) copy-start(bf16[6,128,256]{2,0,1:T(8,128)(2,1)} %get-tuple-element.291) | copy-start | bytes 1179652 | tf_op jit(solution)/shard_map/while
  50.2 0.9 %copy-start.2 = (bf16[2,128,256]{2,1,0:T(8,128)(2,1)S(1)}, bf16[2,128,256]{2,1,0:T(8,128)(2,1)}, u32[]{:S(2)}) copy-start(bf16[2,128,256]{2,1,0:T(8,128)(2,1)} %get-tuple-element.288) | copy-start | bytes 393220 | tf_op jit(solution)/shard_map/while
  50.2 1.0 %copy-start.3 = (bf16[2,128,256]{2,1,0:T(8,128)(2,1)S(1)}, bf16[2,128,256]{2,1,0:T(8,128)(2,1)}, u32[]{:S(2)}) copy-start(bf16[2,128,256]{2,1,0:T(8,128)(2,1)} %get-tuple-element.290) | copy-start | bytes 393220 | tf_op jit(solution)/shard_map/while
  51.2 1.0 %copy-start = (bf16[6,128,256]{2,0,1:T(8,128)(2,1)S(1)}, bf16[6,128,256]{2,0,1:T(8,128)(2,1)}, u32[]{:S(2)}) copy-start(bf16[6,128,256]{2,0,1:T(8,128)(2,1)} %get-tuple-element.289) | copy-start | bytes 1179652 | tf_op jit(solution)/shard_map/while
  60.9 1.2 %copy-start.5 = (f32[2,24]{1,0:T(2,128)S(1)}, f32[2,24]{1,0:T(2,128)}, u32[]{:S(2)}) copy-start(f32[2,24]{1,0:T(2,128)} %copy-done.4) | copy-start | bytes 580 | tf_op jit(solution)/shard_map/while
  62.7 8.8 %collective-permute-start.8 = (bf16[2,3,128]{2,0,1:T(2,128)(2,1)S(1)}, bf16[2,3,128]{2,0,1:T(2,128)(2,1)S(1)}, u32[]{:S(2)}, u32[]{:S(2)}) collective-permute-start(bf16[2,3,128]{2,0,1:T(2,128)(2,1)S(1)} %get-tuple-element.156), channel_id=1, source_target_pairs={{254,0},{0,2},{2,4},{4,6},{6,8},{8,10},{10,12},{12,14},{14,16},{16... | collective-permute-start | bytes 4616 | tf_op jit(solution)/shard_map/ppermute | solution.py:16
  62.8 8.7 %collective-permute-start.9 = (bf16[2,3,128]{2,0,1:T(2,128)(2,1)S(1)}, bf16[2,3,128]{2,0,1:T(2,128)(2,1)S(1)}, u32[]{:S(2)}, u32[]{:S(2)}) collective-permute-start(bf16[2,3,128]{2,0,1:T(2,128)(2,1)S(1)} %get-tuple-element.157), channel_id=1, source_target_pairs={{0,1},{2,3},{4,5},{6,7},{8,9},{10,11},{12,13},{14,15},{16,17},{18,... | collective-permute-start | bytes 4616 | tf_op jit(solution)/shard_map/ppermute | solution.py:22
  65.4 10.2 %collective-permute-start.6 = (bf16[2,128,256]{2,1,0:T(8,128)(2,1)S(1)}, bf16[2,128,256]{2,1,0:T(8,128)(2,1)S(1)}, u32[]{:S(2)}, u32[]{:S(2)}) collective-permute-start(bf16[2,128,256]{2,1,0:T(8,128)(2,1)S(1)} %get-tuple-element.154), channel_id=1, source_target_pairs={{254,0},{0,2},{2,4},{4,6},{6,8},{8,10},{10,12},{12,14},{14,16},{16... | collective-permute-start | bytes 393224 | tf_op jit(solution)/shard_map/ppermute | solution.py:16
  65.8 9.7 %collective-permute-start.7 = (bf16[2,128,256]{2,1,0:T(8,128)(2,1)S(1)}, bf16[2,128,256]{2,1,0:T(8,128)(2,1)S(1)}, u32[]{:S(2)}, u32[]{:S(2)}) collective-permute-start(bf16[2,128,256]{2,1,0:T(8,128)(2,1)S(1)} %get-tuple-element.155), channel_id=1, source_target_pairs={{0,1},{2,3},{4,5},{6,7},{8,9},{10,11},{12,13},{14,15},{16,17},{18,... | collective-permute-start | bytes 393224 | tf_op jit(solution)/shard_map/ppermute | solution.py:22
where the time goes:
time: 77.6 us; the launch traced here: 76.3 us
  other arithmetic  19.7 us (25%)
  starting transfers between devices  19.4 us (25%)
  matrix products  17.7 us (23%)
  waiting for transfers between devices  10.1 us (13%)
  local copies, waits for them, and re-layouts  8.34 us (11%)
    ppermute x5, starting transfers between devices, from_behind(): return lax.ppermute(block, axis, route)  10.1 us
    ppermute x5, starting transfers between devices, passed_along(): return lax.ppermute(value, axis, pairs)  9.29 us
    convert_element_type x2, other arithmetic, pairwise_terms(): kernel = (scaled_terms * screen / radius).astype(jnp.bfloat16)  7.97 us
    ppermute x5, waiting for transfers between devices, from_behind(): return lax.ppermute(block, axis, route)  7.88 us
    dot_general x4, matrix products, spread_rows(): jnp.einsum('tp,t...->p...', selector, values, precision=lax.Precision.HIG...  6.36 us
    dot_general x2, matrix products, pairwise_terms(): jnp.einsum('txc,tyc->txy', nearby_cotangent, remote_features, preferred_e...  3.65 us
    dot_general x6, matrix products, pick_rows(): jnp.einsum('tp,p...->t...', selector, pool, preferred_element_type=jnp.fl...  2.95 us
    unnamed x3, local copies, waits for them, and re-layouts  2.77 us
  transfers between devices with their start and end apart: 10, of which 3 were waited for; matrix products, arithmetic and copies ran while one was open for 9% of the time, Pallas kernels for 0%

commit v1 on v0

v1 whole, which is shorter than its diff:
```python
import math

import jax
import jax.numpy as jnp
from jax import lax
from jax.experimental import pallas as pl
from jax.experimental.pallas import tpu as pltpu
from jax.sharding import PartitionSpec as P

coupling_strength = 0.0625
screening = 0.3
soften = 1.0

AXES = ("gx", "gy", "gz")
MESH = pl.DeviceIdType.MESH
F32, BF16 = jnp.float32, jnp.bfloat16
ROWS = 32

SHIFT = 2.5
SCALED_ERFC = (
    1.0540318489074707, 0.8046519160270691, 0.4539143443107605, 0.171249657869339,
    0.028358077630400658, -0.008383735083043575, -0.004801364149898291, 0.0004147369763813913,
    0.0006639317725785077, -2.737039358180482e-05, -7.203718996606767e-05,
)

OWN, NEXT, PREV, PAIR = "own", "next", "prev", "pair"
TILES = (
    (0, PAIR, 0), (0, PAIR, 1), (0, NEXT, 0), (0, PREV, 0), (0, PREV, 1), (0, OWN, 1),
    (1, PAIR, 0), (1, PAIR, 1), (1, NEXT, 0),
)
SLOT = {tile: n for n, tile in enumerate(TILES)}


def scaled_erfc(x):
    u = 1.0 / (x + SHIFT)
    v = (2.0 * SHIFT) * u - 1.0
    total = jnp.full_like(v, SCALED_ERFC[-1])
    for coefficient in SCALED_ERFC[-2::-1]:
        total = total * v + coefficient
    return total * u


def nt(a, b):
    return lax.dot_general(a, b, (((1,), (1,)), ((), ())), preferred_element_type=F32)


def nn(a, b):
    return lax.dot_general(a, b, (((1,), (0,)), ((), ())), preferred_element_type=F32)


def tn(a, b):
    return lax.dot_general(a, b, (((0,), (0,)), ((), ())), preferred_element_type=F32)


def body(
    gx_size, gy_size,
    feat_hbm, cot_hbm, pos_hbm, elem_hbm, table_ref, part_hbm, flag_hbm,
    out_feat, out_pos,
    feat, cot, pos, elem, part, flag,
    n_feat, n_cot, n_pos, n_elem,
    p_feat, p_cot, p_pos, p_elem, p_part, p_flag,
    z_cot, z_pos, z_elem, z_part, z_flag,
    z_give, z_take,
    wide, kernels, slopes,
    local_sems, send_sems, recv_sems,
):
    gx, gy, gz = lax.axis_index("gx"), lax.axis_index("gy"), lax.axis_index("gz")
    lanes = gx_size * gy_size
    lateral = gx * gy_size + gy
    after = lax.rem(lateral + 1, lanes)
    before = lax.rem(lateral + lanes - 1, lanes)
    next_id = (after // gy_size, lax.rem(after, gy_size), gz)
    prev_id = (before // gy_size, lax.rem(before, gy_size), gz)
    pair_id = (gx, gy, 1 - gz)
    device = lateral * 2 + gz

    barrier = pltpu.get_barrier_semaphore()
    for target in (next_id, prev_id, pair_id):
        pl.semaphore_signal(barrier, inc=1, device_id=target, device_id_type=MESH)

    local = []
    for n, (source, held) in enumerate(
        ((pos_hbm, pos), (elem_hbm, elem), (part_hbm, part), (flag_hbm, flag), (cot_hbm, cot), (feat_hbm, feat))
    ):
        copy = pltpu.make_async_copy(source, held, local_sems.at[n])
        copy.start()
        local.append(copy)

    pl.semaphore_wait(barrier, 3)

    sends = []

    def send(source, held, target):
        n = len(sends)
        copy = pltpu.make_async_remote_copy(
            src_ref=source, dst_ref=held, send_sem=send_sems.at[n], recv_sem=recv_sems.at[n],
            device_id=target, device_id_type=MESH,
        )
        copy.start()
        sends.append(copy)
        return copy

    pair_small = [
        send(pos_hbm, z_pos, pair_id), send(elem_hbm, z_elem, pair_id),
        send(part_hbm, z_part, pair_id), send(flag_hbm, z_flag, pair_id),
    ]
    prev_small = [
        send(pos_hbm, p_pos, next_id), send(elem_hbm, p_elem, next_id),
        send(part_hbm, p_part, next_id), send(flag_hbm, p_flag, next_id),
    ]
    next_small = [send(pos_hbm, n_pos, prev_id), send(elem_hbm, n_elem, prev_id)]
    pair_big = [send(cot_hbm, z_cot, pair_id)]
    next_big = [send(cot_hbm.at[0], n_cot, prev_id), send(feat_hbm.at[0], n_feat, prev_id)]
    prev_big = [send(cot_hbm, p_cot, next_id), send(feat_hbm, p_feat, next_id)]

    def rows_of(pos_ref, elem_ref):
        kinds = elem_ref[...]
        charge = jnp.zeros(kinds.shape, F32)
        for e in range(table_ref.shape[0]):
            charge = charge + jnp.where(kinds == e, table_ref[e], 0.0)
        charge = charge.astype(BF16).astype(F32)
        return [pos_ref[k].astype(F32) for k in range(3)] + [charge]

    def count(part_ref, flag_ref, cluster):
        hit = jnp.where(part_ref[...] == cluster, flag_ref[...].astype(F32), 0.0)
        return jnp.sum(hit, axis=1, keepdims=True)

    for copy in local[:4]:
        copy.wait()
    mine = rows_of(pos, elem)
    stack = jnp.concatenate(
        [mine[k][i : i + 1] for i in range(2) for k in range(4)] + [jnp.zeros((120, 128), F32)], axis=0
    )
    columns = jnp.transpose(stack)
    for i in range(2):
        for k in range(4):
            n = i * 4 + k
            wide[i, k] = jnp.broadcast_to(columns[:, n : n + 1], (128, 128))

    def geometry(tile, rows, factor):
        i, _, j = tile
        slot = SLOT[tile]
        y = [rows[k][j : j + 1] for k in range(3)]
        scaled = rows[3][j : j + 1] * (coupling_strength * factor)

        def chunk(c, carry):
            here = pl.ds(c * ROWS, ROWS)
            dx = wide[i, 0, here, :] - y[0]
            dy = wide[i, 1, here, :] - y[1]
            dz = wide[i, 2, here, :] - y[2]
            r2 = (dx * dx + dy * dy + dz * dz) + soften
            inverse = lax.rsqrt(r2)
            fall = jnp.exp((-screening * screening) * r2)
            ratio = scaled_erfc(screening * (r2 * inverse)) * inverse
            term = (wide[i, 3, here, :] * scaled) * fall
            kernels[slot, here, :] = (term * ratio).astype(BF16)
            slopes[slot, here, :] = -(term * (inverse * inverse)) * (2.0 * screening / math.sqrt(math.pi) + ratio)
            return carry

        lax.fori_loop(0, 128 // ROWS, chunk, 0, unroll=True)

    def padded(rows, j):
        return jnp.concatenate(
            [rows[k][j : j + 1] for k in range(3)] + [jnp.ones((1, 128), F32), jnp.zeros((4, 128), F32)], axis=0
        )

    mine8 = [padded(mine, i) for i in range(2)]
    mine8h = [m.astype(BF16) for m in mine8]

    def weight(tile, pair):
        w = slopes[SLOT[tile]] * pair
        high = w.astype(BF16)
        return high, (w - high.astype(F32)).astype(BF16)

    def to_mine(i, w, other8h):
        s = nt(other8h, w[0]) + nt(other8h, w[1])
        return mine8[i] * s[3:4] - s

    def to_other(i, w, other8):
        s = nn(mine8h[i], w[0]) + nn(mine8h[i], w[1])
        return other8 * s[3:4] - s

    counts = count(part, flag, device * 2 + 1)
    counts0 = count(part, flag, device * 2)
    own = (0, OWN, 1)
    geometry(own, mine, counts[0:1] + counts0[1:2])
    for copy in local[4:]:
        copy.wait()
    w = weight(own, nt(cot[0], feat[1]) + nt(feat[0], cot[1]))
    pos_total = [to_mine(0, w, mine8h[1]), to_other(0, w, mine8[1])]
    kernel = kernels[SLOT[own]]
    feat_total = [nn(kernel, cot[1]), tn(kernel, cot[0])]

    for copy in pair_small:
        copy.wait_recv()
    theirs = rows_of(z_pos, z_elem)
    upper = (device + 1) * 2
    low = [count(part, flag, upper + j) for j in range(2)]
    high = [count(z_part, z_flag, device * 2 + i) for i in range(2)]
    for i in range(2):
        for j in range(2):
            factor = jnp.where(gz == 0, low[j][i : i + 1], high[i][j : j + 1])
            geometry((i, PAIR, j), theirs, factor)
    theirs8 = [padded(theirs, j) for j in range(2)]
    theirs8h = [m.astype(BF16) for m in theirs8]

    for copy in next_small:
        copy.wait_recv()
    side = rows_of(n_pos, n_elem)
    side_counts = count(part, flag, (after * 2 + gz) * 2)
    for i in range(2):
        geometry((i, NEXT, 0), side, side_counts[i : i + 1])
    side8h = padded(side, 0).astype(BF16)

    for copy in prev_small:
        copy.wait_recv()
    back = rows_of(p_pos, p_elem)
    back_counts = count(p_part, p_flag, device * 2)
    for j in range(2):
        geometry((0, PREV, j), back, back_counts[j : j + 1])
    back8h = [padded(back, j).astype(BF16) for j in range(2)]

    for copy in pair_big:
        copy.wait_recv()
    give = [None, None]
    for i in range(2):
        for j in range(2):
            tile = (i, PAIR, j)
            w = weight(tile, nt(feat[i], z_cot[j]))
            pos_total[i] = pos_total[i] + to_mine(i, w, theirs8h[j])
            term = to_other(i, w, theirs8[j])
            give[j] = term if give[j] is None else give[j] + term
            feat_total[i] = feat_total[i] + nn(kernels[SLOT[tile]], z_cot[j])
    for j in range(2):
        z_give[j] = give[j]
    pos_back = send(z_give, z_take, pair_id)

    for copy in next_big:
        copy.wait_recv()
    for i in range(2):
        tile = (i, NEXT, 0)
        w = weight(tile, nt(cot[i], n_feat[...]) + nt(feat[i], n_cot[...]))
        pos_total[i] = pos_total[i] + to_mine(i, w, side8h)
        feat_total[i] = feat_total[i] + nn(kernels[SLOT[tile]], n_cot[...])
    out_feat[1] = feat_total[1]

    for copy in prev_big:
        copy.wait_recv()
    for j in range(2):
        tile = (0, PREV, j)
        w = weight(tile, nt(cot[0], p_feat[j]) + nt(feat[0], p_cot[j]))
        pos_total[0] = pos_total[0] + to_mine(0, w, back8h[j])
        feat_total[0] = feat_total[0] + nn(kernels[SLOT[tile]], p_cot[j])
    out_feat[0] = feat_total[0]

    pos_back.wait_recv()
    for k in range(3):
        out_pos[k] = jnp.concatenate(
            [pos_total[i][k : k + 1] + z_take[i, k : k + 1] for i in range(2)], axis=0
        )
    for copy in sends:
        copy.wait_send()


def per_device(gx_size, gy_size, features, cotangent, positions, element_types, charge_table, partners, tile_real_flags):
    anywhere = pl.BlockSpec(memory_space=pl.ANY)
    inside = pl.BlockSpec(memory_space=pltpu.VMEM)
    clusters, atoms, channels = features.shape
    listed = partners.shape[1]
    big = (clusters, atoms, channels)
    small_pos = pltpu.VMEM((3, clusters, atoms), BF16)
    small_int = pltpu.VMEM((clusters, atoms), jnp.int32)
    lists = pltpu.VMEM((clusters, listed), jnp.int32)
    count = 16
    grad_feat, grad_pos = pl.pallas_call(
        lambda *refs: body(gx_size, gy_size, *refs),
        out_shape=(
            jax.ShapeDtypeStruct(big, F32),
            jax.ShapeDtypeStruct((3, clusters, atoms), F32),
        ),
        in_specs=[anywhere] * 4 + [pl.BlockSpec(memory_space=pltpu.SMEM)] + [anywhere] * 2,
        out_specs=(inside, inside),
        scratch_shapes=[
            pltpu.VMEM(big, BF16), pltpu.VMEM(big, BF16), small_pos, small_int, lists, lists,
            pltpu.VMEM(big[1:], BF16), pltpu.VMEM(big[1:], BF16), small_pos, small_int,
            pltpu.VMEM(big, BF16), pltpu.VMEM(big, BF16), small_pos, small_int, lists, lists,
            pltpu.VMEM(big, BF16), small_pos, small_int, lists, lists,
            pltpu.VMEM((clusters, 8, atoms), F32), pltpu.VMEM((clusters, 8, atoms), F32),
            pltpu.VMEM((clusters, 4, atoms, atoms), F32),
            pltpu.VMEM((len(TILES), atoms, atoms), BF16),
            pltpu.VMEM((len(TILES), atoms, atoms), F32),
            pltpu.SemaphoreType.DMA((6,)),
            pltpu.SemaphoreType.DMA((count,)),
            pltpu.SemaphoreType.DMA((count,)),
        ],
        compiler_params=pltpu.CompilerParams(collective_id=0, has_side_effects=True),
    )(features, cotangent, jnp.transpose(positions, (1, 0, 2)), element_types, charge_table, partners, tile_real_flags)
    return grad_feat, jnp.transpose(grad_pos, (1, 0, 2))


def solution(mesh):
    def run(*args):
        return per_device(mesh.shape["gx"], mesh.shape["gy"], *args)

    return jax.shard_map(
        run,
        mesh=mesh,
        in_specs=(
            P(AXES, None, None),
            P(AXES, None, None),
            P(AXES, None, None),
            P(AXES, None),
            P(),
            P(AXES, None),
            P(AXES, None),
        ),
        out_specs=(P(AXES, None, None), P(AXES, None, None)),
        check_vma=False,
    )
```

time: 77.6 us -> 22.1 us (0.28); the launches traced: 76.3 us -> 21.9 us
  other arithmetic: 19.7 us -> 0 us
  starting transfers between devices: 19.4 us -> 0 us
  Pallas kernels: 0 us -> 19 us
  matrix products: 17.7 us -> 0 us
  waiting for transfers between devices: 10.1 us -> 0 us
  local copies, waits for them, and re-layouts: 8.34 us -> 2.25 us
    ppermute x10 -> x0, starting transfers between devices: 19.4 us -> none  [the longest x5 10.1 us: from_behind(): return lax.ppermute(block, axis, route)]
    pallas_call x0 -> x1, Pallas kernels: none -> 19 us  [per_device(): pl.pallas_call(lambda *refs: body(gx_size, gy_size, *refs), out_shape=(ja...]
    dot_general x18 -> x0, matrix products: 17.7 us -> none  [the longest x4 6.36 us: spread_rows(): jnp.einsum('tp,t...->p...', selector, values, precision=lax.Precision.HIG...]
    ppermute x10 -> x0, waiting for transfers between devices: 10.1 us -> none  [the longest x5 7.88 us: from_behind(): return lax.ppermute(block, axis, route)]
    convert_element_type x5 -> x0, other arithmetic: 8.68 us -> none  [the longest x2 7.97 us: pairwise_terms(): kernel = (scaled_terms * screen / radius).astype(jnp.bfloat16)]
    reduce_sum x5 -> x0, other arithmetic: 4.03 us -> none  [the longest x2 2.09 us: cluster_step(): jnp.sum(pairwise_gradient[2], axis=0)]
    dynamic_update_slice x4 -> x0, local copies, waits for them, and re-layouts: 2.58 us -> none  [per_device(): lax.scan(cluster_step, (start_feat, start_pos), (features, cotangent, pos...]
    concatenate x4 -> x0, other arithmetic: 2.48 us -> none  [the longest x1 1.23 us: per_device(): feat_pool = jnp.concatenate([features, lateral_in[0], upper_in[0]], axis=0)]
  transfers between devices with their start and end apart: 10 -> 0, of which waited for: 3 -> 0; matrix products, arithmetic and copies ran while one was open for 9% -> 0% of each run, Pallas kernels for 0% -> 0%
where the time goes in v1:
time: 22.1 us; the launch traced here: 21.9 us
  Pallas kernels  19 us (86%)
  local copies, waits for them, and re-layouts  2.25 us (10%)
  between operations  0.65 us (3%)
    pallas_call x1, Pallas kernels, per_device(): pl.pallas_call(lambda *refs: body(gx_size, gy_size, *refs), out_shape=(ja...  19 us
    unnamed x4, local copies, waits for them, and re-layouts  2.25 us

profile of v1, /device:TPU:2, one launch (start us, length us, event | category | flops | bytes accessed | tf_op | source)
XLA Modules:
  0.0 21.9 jit_solution(6012541275482597306)
XLA Ops:
  0.6 19.0 %shard_map.86 = (f32[2,128,256]{2,1,0:T(8,128)}, f32[3,2,128]{2,1,0:T(2,128)}) custom-call(bf16[2,128,256]{2,1,0:T(8,128)(2,1)} %refs_0_.1, bf16[2,128,256]{2,1,0:T(8,128)(2,1)} %refs_1_.1, bf16[3,2,128]{2,1,0:T(2,128)(2,1)} %bitcast.3, s32[2,128]{1,0:T(2,128)} %refs_3_.1, f32[8]{0:T(128)} %refs_4_.1, s32[2,24]{1,0:T(2,128)} %refs_5_.1, s32[2,24]{1,0:T(2,128)} %refs_6_.1), custom_call_target="tpu_custom_call" | custom-call | tf_op jit(solution)/shard_map/pallas_call | solution.py:275
  19.7 0.0 copy-start
  19.7 1.7 %copy.11 = f32[2,128,256]{2,1,0:T(8,128)} copy(f32[2,128,256]{2,1,0:T(8,128)} %get-tuple-element.8) | data formatting | bytes 524288
  21.4 0.0 copy-done
  21.4 0.6 %copy.12 = f32[2,3,128]{2,0,1:T(2,128)} copy(f32[2,3,128]{2,0,1:T(2,128)S(1)} %bitcast.2) | data formatting | bytes 6144
Async XLA Ops:
  19.7 1.7 %copy-start = (f32[3,2,128]{2,1,0:T(2,128)S(1)}, f32[3,2,128]{2,1,0:T(2,128)}, u32[]{:S(2)}) copy-start(f32[3,2,128]{2,1,0:T(2,128)} %get-tuple-element.5) | copy-start | bytes 9220

commit v2 on v1

--- a/solution.py
+++ b/solution.py
@@ -61,8 +61,8 @@
     p_feat, p_cot, p_pos, p_elem, p_part, p_flag,
     z_cot, z_pos, z_elem, z_part, z_flag,
     z_give, z_take,
-    wide, kernels, slopes,
-    local_sems, send_sems, recv_sems,
+    wide, kernels, slopes, totals,
+    local_sems, send_sems, recv_sems, entered,
 ):
     gx, gy, gz = lax.axis_index("gx"), lax.axis_index("gy"), lax.axis_index("gz")
     lanes = gx_size * gy_size
@@ -74,8 +74,10 @@
     pair_id = (gx, gy, 1 - gz)
     device = lateral * 2 + gz
 
+    late = lax.rem(lateral, lanes // 2) == 0
+
     barrier = pltpu.get_barrier_semaphore()
-    for target in (next_id, prev_id, pair_id):
+    for target in (prev_id, pair_id):
         pl.semaphore_signal(barrier, inc=1, device_id=target, device_id_type=MESH)
 
     local = []
@@ -86,32 +88,40 @@
         copy.start()
         local.append(copy)
 
-    pl.semaphore_wait(barrier, 3)
+    pl.semaphore_wait(barrier, 2)
+    pl.semaphore_signal(entered, inc=1, device_id=next_id, device_id_type=MESH)
 
     sends = []
 
-    def send(source, held, target):
+    def remote(source, held, target):
         n = len(sends)
         copy = pltpu.make_async_remote_copy(
             src_ref=source, dst_ref=held, send_sem=send_sems.at[n], recv_sem=recv_sems.at[n],
             device_id=target, device_id_type=MESH,
         )
-        copy.start()
         sends.append(copy)
         return copy
 
+    prev_small = [
+        remote(pos_hbm, p_pos, next_id), remote(elem_hbm, p_elem, next_id),
+        remote(part_hbm, p_part, next_id), remote(flag_hbm, p_flag, next_id),
+    ]
     pair_small = [
-        send(pos_hbm, z_pos, pair_id), send(elem_hbm, z_elem, pair_id),
-        send(part_hbm, z_part, pair_id), send(flag_hbm, z_flag, pair_id),
+        remote(pos_hbm, z_pos, pair_id), remote(elem_hbm, z_elem, pair_id),
+        remote(part_hbm, z_part, pair_id), remote(flag_hbm, z_flag, pair_id),
     ]
-    prev_small = [
-        send(pos_hbm, p_pos, next_id), send(elem_hbm, p_elem, next_id),
-        send(part_hbm, p_part, next_id), send(flag_hbm, p_flag, next_id),
-    ]
-    next_small = [send(pos_hbm, n_pos, prev_id), send(elem_hbm, n_elem, prev_id)]
-    pair_big = [send(cot_hbm, z_cot, pair_id)]
-    next_big = [send(cot_hbm.at[0], n_cot, prev_id), send(feat_hbm.at[0], n_feat, prev_id)]
-    prev_big = [send(cot_hbm, p_cot, next_id), send(feat_hbm, p_feat, next_id)]
+    prev_big = [remote(cot_hbm, p_cot, next_id), remote(feat_hbm, p_feat, next_id)]
+    pair_big = [remote(cot_hbm, z_cot, pair_id)]
+    next_small = [remote(pos_hbm, n_pos, prev_id), remote(elem_hbm, n_elem, prev_id)]
+    next_big = [remote(cot_hbm.at[0], n_cot, prev_id), remote(feat_hbm.at[0], n_feat, prev_id)]
+    pos_back = remote(z_give, z_take, pair_id)
+    for copy in prev_small + pair_small + prev_big + pair_big:
+        copy.start()
+
+    def send_back():
+        pl.semaphore_wait(entered, 1)
+        for copy in next_small + next_big:
+            copy.start()
 
     def rows_of(pos_ref, elem_ref):
         kinds = elem_ref[...]
@@ -187,9 +197,13 @@
     for copy in local[4:]:
         copy.wait()
     w = weight(own, nt(cot[0], feat[1]) + nt(feat[0], cot[1]))
-    pos_total = [to_mine(0, w, mine8h[1]), to_other(0, w, mine8[1])]
+    totals[0] = to_mine(0, w, mine8h[1])
+    totals[1] = to_other(0, w, mine8[1])
     kernel = kernels[SLOT[own]]
-    feat_total = [nn(kernel, cot[1]), tn(kernel, cot[0])]
+    out_feat[0] = nn(kernel, cot[1])
+    out_feat[1] = tn(kernel, cot[0])
+
+    pl.when(jnp.logical_not(late))(send_back)
 
     for copy in pair_small:
         copy.wait_recv()
@@ -203,6 +217,18 @@
             geometry((i, PAIR, j), theirs, factor)
     theirs8 = [padded(theirs, j) for j in range(2)]
     theirs8h = [m.astype(BF16) for m in theirs8]
+    for copy in pair_big:
+        copy.wait_recv()
+    for j in range(2):
+        give = []
+        for i in range(2):
+            tile = (i, PAIR, j)
+            w = weight(tile, nt(feat[i], z_cot[j]))
+            totals[i] += to_mine(i, w, theirs8h[j])
+            give.append(to_other(i, w, theirs8[j]))
+            out_feat[i] += nn(kernels[SLOT[tile]], z_cot[j])
+        z_give[j] = give[0] + give[1]
+    pos_back.start()
 
     for copy in next_small:
         copy.wait_recv()
@@ -211,6 +237,15 @@
     for i in range(2):
         geometry((i, NEXT, 0), side, side_counts[i : i + 1])
     side8h = padded(side, 0).astype(BF16)
+    for copy in next_big:
+        copy.wait_recv()
+    for i in range(2):
+        tile = (i, NEXT, 0)
+        w = weight(tile, nt(cot[i], n_feat[...]) + nt(feat[i], n_cot[...]))
+        totals[i] += to_mine(i, w, side8h)
+        out_feat[i] += nn(kernels[SLOT[tile]], n_cot[...])
+
+    pl.when(late)(send_back)
 
     for copy in prev_small:
         copy.wait_recv()
@@ -219,47 +254,30 @@
     for j in range(2):
         geometry((0, PREV, j), back, back_counts[j : j + 1])
     back8h = [padded(back, j).astype(BF16) for j in range(2)]
-
-    for copy in pair_big:
-        copy.wait_recv()
-    give = [None, None]
-    for i in range(2):
-        for j in range(2):
-            tile = (i, PAIR, j)
-            w = weight(tile, nt(feat[i], z_cot[j]))
-            pos_total[i] = pos_total[i] + to_mine(i, w, theirs8h[j])
-            term = to_other(i, w, theirs8[j])
-            give[j] = term if give[j] is None else give[j] + term
-            feat_total[i] = feat_total[i] + nn(kernels[SLOT[tile]], z_cot[j])
-    for j in range(2):
-        z_give[j] = give[j]
-    pos_back = send(z_give, z_take, pair_id)
-
-    for copy in next_big:
-        copy.wait_recv()
-    for i in range(2):
-        tile = (i, NEXT, 0)
-        w = weight(tile, nt(cot[i], n_feat[...]) + nt(feat[i], n_cot[...]))
-        pos_total[i] = pos_total[i] + to_mine(i, w, side8h)
-        feat_total[i] = feat_total[i] + nn(kernels[SLOT[tile]], n_cot[...])
-    out_feat[1] = feat_total[1]
-
+    pos_back.wait_recv()
     for copy in prev_big:
         copy.wait_recv()
+    pos_total = [totals[i] + z_take[i] for i in range(2)]
     for j in range(2):
         tile = (0, PREV, j)
         w = weight(tile, nt(cot[0], p_feat[j]) + nt(feat[0], p_cot[j]))
         pos_total[0] = pos_total[0] + to_mine(0, w, back8h[j])
-        feat_total[0] = feat_total[0] + nn(kernels[SLOT[tile]], p_cot[j])
-    out_feat[0] = feat_total[0]
-
-    pos_back.wait_recv()
+    out_feat[0] += nn(kernels[SLOT[(0, PREV, 0)]], p_cot[0]) + nn(kernels[SLOT[(0, PREV, 1)]], p_cot[1])
     for k in range(3):
-        out_pos[k] = jnp.concatenate(
-            [pos_total[i][k : k + 1] + z_take[i, k : k + 1] for i in range(2)], axis=0
-        )
+        out_pos[k] = jnp.concatenate([pos_total[i][k : k + 1] for i in range(2)], axis=0)
     for copy in sends:
         copy.wait_send()
+
+
+def store(feat_ref, pos_ref, out_feat, out_pos, sems):
+    copies = [
+        pltpu.make_async_copy(feat_ref, out_feat, sems.at[0]),
+        pltpu.make_async_copy(pos_ref, out_pos, sems.at[1]),
+    ]
+    for copy in copies:
+        copy.start()
+    for copy in copies:
+        copy.wait()
 
 
 def per_device(gx_size, gy_size, features, cotangent, positions, element_types, charge_table, partners, tile_real_flags):
@@ -275,8 +293,8 @@
     grad_feat, grad_pos = pl.pallas_call(
         lambda *refs: body(gx_size, gy_size, *refs),
         out_shape=(
-            jax.ShapeDtypeStruct(big, F32),
-            jax.ShapeDtypeStruct((3, clusters, atoms), F32),
+            pltpu.VMEM(big, F32),
+            pltpu.VMEM((3, clusters, atoms), F32),
         ),
         in_specs=[anywhere] * 4 + [pl.BlockSpec(memory_space=pltpu.SMEM)] + [anywhere] * 2,
         out_specs=(inside, inside),
@@ -289,12 +307,24 @@
             pltpu.VMEM((clusters, 4, atoms, atoms), F32),
             pltpu.VMEM((len(TILES), atoms, atoms), BF16),
             pltpu.VMEM((len(TILES), atoms, atoms), F32),
+            pltpu.VMEM((clusters, 8, atoms), F32),
             pltpu.SemaphoreType.DMA((6,)),
             pltpu.SemaphoreType.DMA((count,)),
             pltpu.SemaphoreType.DMA((count,)),
+            pltpu.SemaphoreType.REGULAR,
         ],
         compiler_params=pltpu.CompilerParams(collective_id=0, has_side_effects=True),
     )(features, cotangent, jnp.transpose(positions, (1, 0, 2)), element_types, charge_table, partners, tile_real_flags)
+    grad_feat, grad_pos = pl.pallas_call(
+        store,
+        out_shape=(
+            jax.ShapeDtypeStruct(big, F32),
+            jax.ShapeDtypeStruct((3, clusters, atoms), F32),
+        ),
+        in_specs=[inside, inside],
+        out_specs=(anywhere, anywhere),
+        scratch_shapes=[pltpu.SemaphoreType.DMA((2,))],
+    )(*[pltpu.with_memory_space_constraint(x, pltpu.VMEM) for x in (grad_feat, grad_pos)])
     return grad_feat, jnp.transpose(grad_pos, (1, 0, 2))
 
 

time: 22.1 us -> 17.4 us (0.79)
  Pallas kernels: 19 us -> 16.7 us
  local copies, waits for them, and re-layouts: 2.25 us -> 0 us
    pallas_call x1 -> x2, Pallas kernels: 19 us -> 16.7 us  [the longest x1 15.9 us: per_device(): pl.pallas_call(lambda *refs: body(gx_size, gy_size, *refs), out_shape=(pl...]
    unnamed x4 -> x0, local copies, waits for them, and re-layouts: 2.25 us -> none
where the time goes in v2:
time: 17.4 us; the launch traced here: 17.3 us
  Pallas kernels  16.7 us (96%)
  between operations  0.64 us (4%)
    pallas_call x1, Pallas kernels, per_device(): pl.pallas_call(lambda *refs: body(gx_size, gy_size, *refs), out_shape=(pl...  15.9 us
    pallas_call x1, Pallas kernels, per_device(): pl.pallas_call(store, out_shape=(jax.ShapeDtypeStruct(big, F32), jax.Shap...  0.72 us

profile of v2, /device:TPU:2, one launch (start us, length us, event | category | flops | bytes accessed | tf_op | source)
XLA Modules:
  0.0 17.3 jit_solution(14508661329843502538)
XLA Ops:
  0.6 15.9 %shard_map.86 = (f32[2,128,256]{2,1,0:T(8,128)S(1)}, f32[3,2,128]{2,1,0:T(2,128)S(1)}) custom-call(bf16[2,128,256]{2,1,0:T(8,128)(2,1)} %refs_0_.1, bf16[2,128,256]{2,1,0:T(8,128)(2,1)} %refs_1_.1, bf16[3,2,128]{2,1,0:T(2,128)(2,1)} %bitcast.2, s32[2,128]{1,0:T(2,128)} %refs_3_.1, f32[8]{0:T(128)} %refs_4_.1, s32[2,24]{1,0:T(2,128)} %refs_5_.1, s32[2,24]{1,0:T(2,128)} %refs_6_.1), custom_call_target="tpu_custom_call" | custom-call | tf_op jit(solution)/shard_map/pallas_call | solution.py:293
  16.6 0.7 %shard_map.87 = (f32[2,128,256]{2,1,0:T(8,128)}, f32[3,2,128]{2,1,0:T(2,128)}) custom-call(f32[2,128,256]{2,1,0:T(8,128)S(1)} %get-tuple-element.6.feat_ref, f32[3,2,128]{2,1,0:T(2,128)S(1)} %get-tuple-element.7.pos_ref), custom_call_target="tpu_custom_call" | custom-call | tf_op jit(solution)/shard_map/pallas_call | solution.py:318

commit v3 on v2

--- a/solution.py
+++ b/solution.py
@@ -54,15 +54,15 @@
 
 def body(
     gx_size, gy_size,
-    feat_hbm, cot_hbm, pos_hbm, elem_hbm, table_ref, part_hbm, flag_hbm,
+    feat_hbm, cot_hbm, pos_hbm, elem_hbm, table_hbm, part_hbm, flag_hbm,
     out_feat, out_pos,
     feat, cot, pos, elem, part, flag,
     n_feat, n_cot, n_pos, n_elem,
     p_feat, p_cot, p_pos, p_elem, p_part, p_flag,
     z_cot, z_pos, z_elem, z_part, z_flag,
     z_give, z_take,
-    wide, kernels, slopes, totals,
-    local_sems, send_sems, recv_sems, entered,
+    wide, kernels, slopes, totals, table_ref,
+    local_sems, send_sems, recv_sems, entered, told,
 ):
     gx, gy, gz = lax.axis_index("gx"), lax.axis_index("gy"), lax.axis_index("gz")
     lanes = gx_size * gy_size
@@ -76,19 +76,25 @@
 
     late = lax.rem(lateral, lanes // 2) == 0
 
+    first = lax.rem(lateral + 1, lanes // 2) == 0
+    teller = lax.rem(lateral + 2, lanes // 2) == 0
+
     barrier = pltpu.get_barrier_semaphore()
-    for target in (prev_id, pair_id):
-        pl.semaphore_signal(barrier, inc=1, device_id=target, device_id_type=MESH)
+    pl.semaphore_signal(barrier, inc=1, device_id=prev_id, device_id_type=MESH)
+
+    @pl.when(jnp.logical_not(first))
+    def _():
+        pl.semaphore_signal(barrier, inc=1, device_id=pair_id, device_id_type=MESH)
 
     local = []
     for n, (source, held) in enumerate(
-        ((pos_hbm, pos), (elem_hbm, elem), (part_hbm, part), (flag_hbm, flag), (cot_hbm, cot), (feat_hbm, feat))
+        ((table_hbm, table_ref), (pos_hbm, pos), (elem_hbm, elem), (part_hbm, part), (flag_hbm, flag), (cot_hbm, cot), (feat_hbm, feat))
     ):
         copy = pltpu.make_async_copy(source, held, local_sems.at[n])
         copy.start()
         local.append(copy)
 
-    pl.semaphore_wait(barrier, 2)
+    pl.semaphore_wait(barrier, jnp.where(first, 1, 2))
     pl.semaphore_signal(entered, inc=1, device_id=next_id, device_id_type=MESH)
 
     sends = []
@@ -115,7 +121,20 @@
     next_small = [remote(pos_hbm, n_pos, prev_id), remote(elem_hbm, n_elem, prev_id)]
     next_big = [remote(cot_hbm.at[0], n_cot, prev_id), remote(feat_hbm.at[0], n_feat, prev_id)]
     pos_back = remote(z_give, z_take, pair_id)
-    for copy in prev_small + pair_small + prev_big + pair_big:
+    for copy in prev_small + prev_big:
+        copy.start()
+
+    @pl.when(teller)
+    def _():
+        pl.semaphore_signal(told, inc=1, device_id=pair_id, device_id_type=MESH)
+        pl.semaphore_wait(told, 1)
+        pl.semaphore_signal(told, inc=1, device_id=next_id, device_id_type=MESH)
+
+    @pl.when(first)
+    def _():
+        pl.semaphore_wait(told, 1)
+
+    for copy in pair_small + pair_big:
         copy.start()
 
     def send_back():
@@ -135,7 +154,7 @@
         hit = jnp.where(part_ref[...] == cluster, flag_ref[...].astype(F32), 0.0)
         return jnp.sum(hit, axis=1, keepdims=True)
 
-    for copy in local[:4]:
+    for copy in local[:5]:
         copy.wait()
     mine = rows_of(pos, elem)
     stack = jnp.concatenate(
@@ -194,7 +213,7 @@
     counts0 = count(part, flag, device * 2)
     own = (0, OWN, 1)
     geometry(own, mine, counts[0:1] + counts0[1:2])
-    for copy in local[4:]:
+    for copy in local[5:]:
         copy.wait()
     w = weight(own, nt(cot[0], feat[1]) + nt(feat[0], cot[1]))
     totals[0] = to_mine(0, w, mine8h[1])
@@ -296,7 +315,7 @@
             pltpu.VMEM(big, F32),
             pltpu.VMEM((3, clusters, atoms), F32),
         ),
-        in_specs=[anywhere] * 4 + [pl.BlockSpec(memory_space=pltpu.SMEM)] + [anywhere] * 2,
+        in_specs=[anywhere] * 7,
         out_specs=(inside, inside),
         scratch_shapes=[
             pltpu.VMEM(big, BF16), pltpu.VMEM(big, BF16), small_pos, small_int, lists, lists,
@@ -308,9 +327,11 @@
             pltpu.VMEM((len(TILES), atoms, atoms), BF16),
             pltpu.VMEM((len(TILES), atoms, atoms), F32),
             pltpu.VMEM((clusters, 8, atoms), F32),
-            pltpu.SemaphoreType.DMA((6,)),
+            pltpu.SMEM(charge_table.shape, F32),
+            pltpu.SemaphoreType.DMA((7,)),
             pltpu.SemaphoreType.DMA((count,)),
             pltpu.SemaphoreType.DMA((count,)),
+            pltpu.SemaphoreType.REGULAR,
             pltpu.SemaphoreType.REGULAR,
         ],
         compiler_params=pltpu.CompilerParams(collective_id=0, has_side_effects=True),

time: 17.4 us -> 16.3 us (0.937)
  Pallas kernels: 16.7 us -> 15.5 us
    pallas_call x1, Pallas kernels: 15.9 us -> 14.8 us  [per_device(): pl.pallas_call(lambda *refs: body(gx_size, gy_size, *refs), out_shape=(pl...]
where the time goes in v3:
time: 16.3 us; the launch traced here: 16.2 us
  Pallas kernels  15.5 us (95%)
  between operations  0.64 us (4%)
    pallas_call x1, Pallas kernels, per_device(): pl.pallas_call(lambda *refs: body(gx_size, gy_size, *refs), out_shape=(pl...  14.8 us
    pallas_call x1, Pallas kernels, per_device(): pl.pallas_call(store, out_shape=(jax.ShapeDtypeStruct(big, F32), jax.Shap...  0.72 us

profile of v3, /device:TPU:2, one launch (start us, length us, event | category | flops | bytes accessed | tf_op | source)
XLA Modules:
  0.0 16.2 jit_solution(12592718654995733726)
XLA Ops:
  0.6 14.8 %shard_map.86 = (f32[2,128,256]{2,1,0:T(8,128)S(1)}, f32[3,2,128]{2,1,0:T(2,128)S(1)}) custom-call(bf16[2,128,256]{2,1,0:T(8,128)(2,1)} %refs_0_.1, bf16[2,128,256]{2,1,0:T(8,128)(2,1)} %refs_1_.1, bf16[3,2,128]{2,1,0:T(2,128)(2,1)} %bitcast.2, s32[2,128]{1,0:T(2,128)} %refs_3_.1, f32[8]{0:T(128)} %refs_4_.1, s32[2,24]{1,0:T(2,128)} %refs_5_.1, s32[2,24]{1,0:T(2,128)} %refs_6_.1), custom_call_target="tpu_custom_call" | custom-call | tf_op jit(solution)/shard_map/pallas_call | solution.py:312
  15.4 0.7 %shard_map.87 = (f32[2,128,256]{2,1,0:T(8,128)}, f32[3,2,128]{2,1,0:T(2,128)}) custom-call(f32[2,128,256]{2,1,0:T(8,128)S(1)} %get-tuple-element.6.feat_ref, f32[3,2,128]{2,1,0:T(2,128)S(1)} %get-tuple-element.7.pos_ref), custom_call_target="tpu_custom_call" | custom-call | tf_op jit(solution)/shard_map/pallas_call | solution.py:339

commit v4 on v3

--- a/solution.py
+++ b/solution.py
@@ -15,6 +15,7 @@
 MESH = pl.DeviceIdType.MESH
 F32, BF16 = jnp.float32, jnp.bfloat16
 ROWS = 32
+PIECES = 2
 
 SHIFT = 2.5
 SCALED_ERFC = (
@@ -60,7 +61,7 @@
     n_feat, n_cot, n_pos, n_elem,
     p_feat, p_cot, p_pos, p_elem, p_part, p_flag,
     z_cot, z_pos, z_elem, z_part, z_flag,
-    z_give, z_take,
+    z_give, z_take, hold,
     wide, kernels, slopes, totals, table_ref,
     local_sems, send_sems, recv_sems, entered, told,
 ):
@@ -79,6 +80,13 @@
     first = lax.rem(lateral + 1, lanes // 2) == 0
     teller = lax.rem(lateral + 2, lanes // 2) == 0
 
+    middle = lax.rem(lateral, lanes // 2) == lanes // 2 - gy_size + 1
+    start = lateral - lax.rem(lateral, lanes // 2)
+    across = lax.rem(start + lanes // 2, lanes)
+
+    def device_at(where):
+        return (where // gy_size, lax.rem(where, gy_size), gz)
+
     barrier = pltpu.get_barrier_semaphore()
     pl.semaphore_signal(barrier, inc=1, device_id=prev_id, device_id_type=MESH)
 
@@ -94,15 +102,24 @@
         copy.start()
         local.append(copy)
 
-    pl.semaphore_wait(barrier, jnp.where(first, 1, 2))
+    @pl.when(middle)
+    def _():
+        pl.semaphore_signal(barrier, inc=1, device_id=device_at(start + lanes // 2 - 1), device_id_type=MESH)
+
+    @pl.when(late)
+    def _():
+        pl.semaphore_signal(barrier, inc=1, device_id=device_at(across + lanes // 2 - gy_size + 1), device_id_type=MESH)
+
+    pl.semaphore_wait(barrier, jnp.where(middle, 3, 2))
     pl.semaphore_signal(entered, inc=1, device_id=next_id, device_id_type=MESH)
 
     sends = []
 
-    def remote(source, held, target):
+    def remote(source, held, target, arrival=None):
         n = len(sends)
         copy = pltpu.make_async_remote_copy(
-            src_ref=source, dst_ref=held, send_sem=send_sems.at[n], recv_sem=recv_sems.at[n],
+            src_ref=source, dst_ref=held, send_sem=send_sems.at[n],
+            recv_sem=recv_sems.at[n if arrival is None else arrival],
             device_id=target, device_id_type=MESH,
         )
         sends.append(copy)
@@ -116,13 +133,34 @@
         remote(pos_hbm, z_pos, pair_id), remote(elem_hbm, z_elem, pair_id),
         remote(part_hbm, z_part, pair_id), remote(flag_hbm, z_flag, pair_id),
     ]
-    prev_big = [remote(cot_hbm, p_cot, next_id), remote(feat_hbm, p_feat, next_id)]
+    prev_big = [remote(cot_hbm, p_cot, next_id), remote(feat_hbm.at[0], p_feat.at[0], next_id)]
     pair_big = [remote(cot_hbm, z_cot, pair_id)]
     next_small = [remote(pos_hbm, n_pos, prev_id), remote(elem_hbm, n_elem, prev_id)]
     next_big = [remote(cot_hbm.at[0], n_cot, prev_id), remote(feat_hbm.at[0], n_feat, prev_id)]
     pos_back = remote(z_give, z_take, pair_id)
+    always = list(sends)
+    pieces = [pl.ds(at, feat.shape[1] // PIECES) for at in range(0, feat.shape[1], feat.shape[1] // PIECES)]
+    relay = device_at(start + lanes // 2 - gy_size + 1)
+    target = device_at(across)
+    base = len(sends)
+    direct = [remote(feat_hbm.at[1, rows], p_feat.at[1, rows], next_id) for rows in pieces]
+    relayed = [remote(feat_hbm.at[1, rows], hold.at[rows], relay) for rows in pieces]
+    handed = [
+        remote(hold.at[rows], p_feat.at[1, rows], target, base + n) for n, rows in enumerate(pieces)
+    ]
+
+    @pl.when(first)
+    def _():
+        for copy in relayed:
+            copy.start()
+
     for copy in prev_small + prev_big:
         copy.start()
+
+    @pl.when(jnp.logical_not(first))
+    def _():
+        for copy in direct:
+            copy.start()
 
     @pl.when(teller)
     def _():
@@ -136,6 +174,12 @@
 
     for copy in pair_small + pair_big:
         copy.start()
+
+    @pl.when(middle)
+    def _():
+        for n, copy in enumerate(relayed):
+            copy.wait_recv()
+            handed[n].start()
 
     def send_back():
         pl.semaphore_wait(entered, 1)
@@ -274,7 +318,7 @@
         geometry((0, PREV, j), back, back_counts[j : j + 1])
     back8h = [padded(back, j).astype(BF16) for j in range(2)]
     pos_back.wait_recv()
-    for copy in prev_big:
+    for copy in prev_big + direct:
         copy.wait_recv()
     pos_total = [totals[i] + z_take[i] for i in range(2)]
     for j in range(2):
@@ -284,8 +328,23 @@
     out_feat[0] += nn(kernels[SLOT[(0, PREV, 0)]], p_cot[0]) + nn(kernels[SLOT[(0, PREV, 1)]], p_cot[1])
     for k in range(3):
         out_pos[k] = jnp.concatenate([pos_total[i][k : k + 1] for i in range(2)], axis=0)
-    for copy in sends:
+    for copy in always:
         copy.wait_send()
+
+    @pl.when(jnp.logical_not(first))
+    def _():
+        for copy in direct:
+            copy.wait_send()
+
+    @pl.when(first)
+    def _():
+        for copy in relayed:
+            copy.wait_send()
+
+    @pl.when(middle)
+    def _():
+        for copy in handed:
+            copy.wait_send()
 
 
 def store(feat_ref, pos_ref, out_feat, out_pos, sems):
@@ -308,7 +367,7 @@
     small_pos = pltpu.VMEM((3, clusters, atoms), BF16)
     small_int = pltpu.VMEM((clusters, atoms), jnp.int32)
     lists = pltpu.VMEM((clusters, listed), jnp.int32)
-    count = 16
+    count = 16 + 3 * PIECES
     grad_feat, grad_pos = pl.pallas_call(
         lambda *refs: body(gx_size, gy_size, *refs),
         out_shape=(
@@ -323,6 +382,7 @@
             pltpu.VMEM(big, BF16), pltpu.VMEM(big, BF16), small_pos, small_int, lists, lists,
             pltpu.VMEM(big, BF16), small_pos, small_int, lists, lists,
             pltpu.VMEM((clusters, 8, atoms), F32), pltpu.VMEM((clusters, 8, atoms), F32),
+            pltpu.VMEM(big[1:], BF16),
             pltpu.VMEM((clusters, 4, atoms, atoms), F32),
             pltpu.VMEM((len(TILES), atoms, atoms), BF16),
             pltpu.VMEM((len(TILES), atoms, atoms), F32),

time: 16.3 us -> 15.7 us (0.963)
  Pallas kernels: 15.5 us -> 15 us
    pallas_call x1, Pallas kernels: 14.8 us -> 14.2 us  [per_device(): pl.pallas_call(lambda *refs: body(gx_size, gy_size, *refs), out_shape=(pl...]
where the time goes in v4:
time: 15.7 us; the launch traced here: 15.6 us
  Pallas kernels  15 us (96%)
  between operations  0.64 us (4%)
    pallas_call x1, Pallas kernels, per_device(): pl.pallas_call(lambda *refs: body(gx_size, gy_size, *refs), out_shape=(pl...  14.2 us
    pallas_call x1, Pallas kernels, per_device(): pl.pallas_call(store, out_shape=(jax.ShapeDtypeStruct(big, F32), jax.Shap...  0.72 us

profile of v4, /device:TPU:2, one launch (start us, length us, event | category | flops | bytes accessed | tf_op | source)
XLA Modules:
  0.0 15.6 jit_solution(13733287623933972335)
XLA Ops:
  0.6 14.2 %shard_map.86 = (f32[2,128,256]{2,1,0:T(8,128)S(1)}, f32[3,2,128]{2,1,0:T(2,128)S(1)}) custom-call(bf16[2,128,256]{2,1,0:T(8,128)(2,1)} %refs_0_.1, bf16[2,128,256]{2,1,0:T(8,128)(2,1)} %refs_1_.1, bf16[3,2,128]{2,1,0:T(2,128)(2,1)} %bitcast.2, s32[2,128]{1,0:T(2,128)} %refs_3_.1, f32[8]{0:T(128)} %refs_4_.1, s32[2,24]{1,0:T(2,128)} %refs_5_.1, s32[2,24]{1,0:T(2,128)} %refs_6_.1), custom_call_target="tpu_custom_call" | custom-call | tf_op jit(solution)/shard_map/pallas_call | solution.py:371
  14.9 0.7 %shard_map.87 = (f32[2,128,256]{2,1,0:T(8,128)}, f32[3,2,128]{2,1,0:T(2,128)}) custom-call(f32[2,128,256]{2,1,0:T(8,128)S(1)} %get-tuple-element.6.feat_ref, f32[3,2,128]{2,1,0:T(2,128)S(1)} %get-tuple-element.7.pos_ref), custom_call_target="tpu_custom_call" | custom-call | tf_op jit(solution)/shard_map/pallas_call | solution.py:399
